TPU v7x, 32 devices: a whole 2x2x4 slice. The times are simulated.
32 devices in a mesh: rows: 16 (over z, y, x), cols: 2 (over core).
Axes of the slice: x: 2, y: 2, z: 4, core: 2. Of those that a mesh axis runs over, the one named last changes fastest.
Arguments:
- row_points: float32 [3, 8192], P(None, 'rows')
- panel_points: bfloat16 [3, 512], P(None, ('rows', 'cols')), may hold values from 0 to 1
- test_vectors: bfloat16 [128, 512], P(None, ('rows', 'cols')), may hold values from -0.25 to 0.25
- leaf_skeleton: int32 [16, 64], P('rows'), may hold values from 0 to 511, as said below
- node_skeleton: int32 [16, 4, 64], P('rows'), may hold values from 0 to 127, as said below
Outputs:
- leaf_interp: float32 [64, 8192], P(None, ('rows', 'cols'))
- transfers: float32 [16, 4, 64, 128], P('rows')
- top_skeleton: float32 [16, 64, 256], P('rows')
Inputs may be any that keep to these rules, and one draw needn't show every extreme that they name: `leaf_skeleton`: each leaf's 64 entries are distinct. `node_skeleton`: each entry list holds 64 distinct positions among the 128 stacked rows (the lower child's first); all leaves under the same node have the same list at that level.
All inputs are finite; a program needn't handle non-finite values.
Results may differ from a plain program's by a relative error of at most 0.0049.
Values may be sent and summed in bfloat16 or wider, within the bound.
No kernel may reach another device: no remote copies, remote signals or barrier semaphores. Data moves between devices by JAX's collectives and lax.ppermute only.
A program may use at most 64 MiB of HBM per device.

v0:
```python
import math
import jax
import jax.numpy as jnp
from jax import lax
from jax.sharding import PartitionSpec as P

KAPPA = 40.0
SMOOTH = 0.05
RIDGE = 0.1
EPSILON = 1e-05


def from_partner(shard, axis, bit):
    return lax.ppermute(shard, axis, [(i, i ^ 1 << bit) for i in range(lax.axis_size(axis))])


def kernel_block(targets, sources):
    source_f = sources.astype(jnp.float32)
    dist_sq = jnp.zeros((targets.shape[1], source_f.shape[1]), jnp.float32)
    for component in range(3):
        offset = targets[component][:, None] - source_f[component][None, :]
        dist_sq = dist_sq + offset * offset
    radius = jnp.sqrt(dist_sq + SMOOTH * SMOOTH)
    real_part = (jnp.cos(KAPPA * radius) / radius).astype(jnp.bfloat16)
    imag_part = (jnp.sin(KAPPA * radius) / radius).astype(jnp.bfloat16)
    return (real_part, imag_part)


def sample_block(real_part, imag_part, vectors):
    first_half = jnp.dot(real_part, vectors.T, preferred_element_type=jnp.float32)
    second_half = jnp.dot(imag_part, vectors.T, preferred_element_type=jnp.float32)
    return jnp.concatenate([first_half, second_half], axis=1)


def interpolate(block, skeleton):
    gram_matrix = jnp.dot(skeleton, skeleton.T, precision=lax.Precision.HIGHEST)
    ridge = RIDGE * skeleton.shape[1] * (jnp.mean(skeleton * skeleton) + EPSILON)
    gram_matrix = gram_matrix + ridge * jnp.eye(skeleton.shape[0], dtype=jnp.float32)
    factor = jnp.linalg.cholesky(gram_matrix)
    right_side = jnp.dot(skeleton, block.T, precision=lax.Precision.HIGHEST)
    middle = lax.linalg.triangular_solve(factor, right_side, left_side=True, lower=True)
    return lax.linalg.triangular_solve(factor, middle, left_side=True, lower=True, transpose_a=True)


def body(row_points, panel_points, test_vectors, leaf_skeleton, node_skeleton):
    rows_here = row_points.shape[1]
    vec_count = test_vectors.shape[0]
    level_count = node_skeleton.shape[1]
    zero_sum = jnp.zeros((rows_here, 2 * vec_count), jnp.float32)
    running = zero_sum
    vectors = lax.all_gather(test_vectors, "rows", axis=1, tiled=True)
    sources = lax.all_gather(panel_points, "rows", axis=1, tiled=True)
    piece_width = vectors.shape[1]
    block_width = math.gcd(piece_width, 512)
    block_count = piece_width // block_width
    vec_blocks = jnp.moveaxis(vectors.reshape(vec_count, block_count, block_width), 1, 0)
    src_blocks = jnp.moveaxis(sources.reshape(3, block_count, block_width), 1, 0)

    def one_block(acc_sum, blocks):
        real_part, imag_part = kernel_block(row_points, blocks[1])
        return (acc_sum + sample_block(real_part, imag_part, blocks[0]), None)

    running, unused = lax.scan(one_block, running, (vec_blocks, src_blocks))
    half_rows = rows_here // lax.axis_size("cols")
    col_index = lax.axis_index("cols")
    samples = lax.psum(running, "cols")
    skel_rows = jnp.take(samples, leaf_skeleton[0], axis=0)
    own_samples = lax.dynamic_slice_in_dim(samples, col_index * half_rows, half_rows, 0)
    leaf_interp = interpolate(own_samples, skel_rows)
    row_index = lax.axis_index("rows")
    current = skel_rows
    level_maps = []
    for tree_level in range(level_count):
        partner = from_partner(current, "rows", tree_level)
        is_upper = jnp.right_shift(row_index, tree_level) & 1 == 1
        lower_child = jnp.where(is_upper, partner, current)
        upper_child = jnp.where(is_upper, current, partner)
        stacked = jnp.concatenate([lower_child, upper_child], axis=0)
        current = jnp.take(stacked, node_skeleton[0, tree_level], axis=0)
        level_maps.append(interpolate(stacked, current))
    path_maps = jnp.stack(level_maps)
    return (leaf_interp, path_maps[None], current[None])


def solution(mesh):
    placed = (
        P(None, "rows"),
        P(None, ("rows", "cols")),
        P(None, ("rows", "cols")),
        P("rows", None),
        P("rows", None, None),
    )
    return jax.shard_map(
        body,
        mesh=mesh,
        in_specs=placed,
        out_specs=(P(None, ("rows", "cols")), P("rows", None, None, None), P("rows", None, None)),
        check_vma=False,
    )
```

profile of v0, /device:TPU:0, one launch (start us, length us, event | category | flops | bytes accessed | tf_op | source)
XLA Modules:
  0.0 203.0 jit_solution(5670295947467593674)
XLA Ops:
  7.2 0.6 copy-done.4
  7.8 42.5 %all-gather = bf16[16,16,3]{1,2,0:T(4,128)(2,1)S(1)} all-gather(bf16[1,16,3]{1,2,0:T(4,128)(2,1)S(1)} %bitcast.136), channel_id=1, replica_groups=mesh['rows'=16,'cols'=2] {'rows'}, dimensions={0}, use_global_device_ids=true | all-gather | bytes 1632 | tf_op jit(solution)/shard_map/all_gather | solution.py:52
  50.4 0.6 copy-done.1
  51.0 0.7 copy-done.2
  51.7 35.8 %all_gather.7 = bf16[128,256]{0,1:T(8,128)(2,1)S(1)} all-gather(bf16[128,16]{0,1:T(8,128)(2,1)S(1)} %copy-done.2), channel_id=1, replica_groups=mesh['rows'=16,'cols'=2] {'rows'}, dimensions={1}, use_global_device_ids=true | all-gather | bytes 69632 | tf_op jit(solution)/shard_map/all_gather | solution.py:51
  87.5 2.4 %fusion = f32[512,128]{0,1:T(8,128)S(1)} fusion(bf16[128,256]{0,1:T(8,128)(2,1)S(1)} %all_gather.7, f32[256]{0:T(256)S(1)} %bitcast.139, f32[512]{0:T(512)S(1)} %bitcast.132, f32[256]{0:T(256)S(1)} %bitcast.141, f32[512]{0:T(512)S(1)} %bitcast.134, f32[256]{0:T(256)S(1)} %bitcast.137, f32[512]{0:T(512)S(1)} %bitcast.130), kind=kOutput, calls=%fused_computation.18 | convolution fusion | flops 35127296 | bytes 336896 | tf_op jit(solution)/shard_map/while/body/eval_jaxpr/dot_general | solution.py:30
  89.9 2.4 %fusion.1 = f32[512,128]{0,1:T(8,128)S(1)} fusion(bf16[128,256]{0,1:T(8,128)(2,1)S(1)} %all_gather.7, f32[256]{0:T(256)S(1)} %bitcast.140, f32[512]{0:T(512)S(1)} %bitcast.133, f32[256]{0:T(256)S(1)} %bitcast.142, f32[512]{0:T(512)S(1)} %bitcast.135, f32[256]{0:T(256)S(1)} %bitcast.138, f32[512]{0:T(512)S(1)} %bitcast.131), kind=kOutput, calls=%fused_computation.19 | convolution fusion | flops 35127296 | bytes 336896 | tf_op jit(solution)/shard_map/while/body/eval_jaxpr/dot_general | solution.py:31
  92.3 0.8 pad_maximum_fusion
  93.1 0.6 copy-done.5
  93.8 0.7 copy-done.3
  94.6 15.1 %all-reduce.2.cloned.1.call-done = f32[512,256]{0,1:T(8,128)} async-done(((f32[512,256]{0,1:T(8,128)}), f32[512,256]{0,1:T(8,128)}) %all-reduce.2.cloned.1.call-update) | async-done | bytes 524304 | tf_op jit(solution)/shard_map/psum | solution.py:66
  109.7 1.2 copy.53
  110.9 0.7 gather_fusion
  111.6 0.7 multiply_reduce_fusion.4
  112.3 1.8 collective-permute-start
  114.7 0.2 convolution_add_fusion.4
  115.0 5.8 %cholesky.89 = f32[64,64]{1,0:T(8,128)S(1)} custom-call(f32[64,64]{1,0:T(8,128)S(1)} %fusion.48), custom_call_target="Cholesky" | custom-call | tf_op jit(solution)/shard_map/jit(cholesky)/cholesky | solution.py:39
  121.0 0.6 compare_reduce_fusion.4
  121.7 0.7 fusion.23
  122.4 4.9 %custom-call.13 = f32[1,64,64]{1,2,0:T(8,128)S(1)} custom-call(f32[1,64,64]{2,1,0:T(8,128)S(1)} %copy.58), custom_call_target="InvertDiagBlocksLowerTriangular" | custom-call | tf_op jit(solution)/shard_map/triangular_solve | solution.py:42
  127.4 0.3 fusion.2
  127.6 0.3 fusion.46
  127.9 0.8 fusion.44
  128.8 0.7 gather_fusion.1
  129.4 0.7 multiply_reduce_fusion.3
  130.1 0.3 fusion.68
  130.4 1.5 collective-permute-start.1
  132.6 0.2 convolution_add_fusion.3
  132.9 5.8 %cholesky.100 = f32[64,64]{1,0:T(8,128)S(1)} custom-call(f32[64,64]{1,0:T(8,128)S(1)} %fusion.43), custom_call_target="Cholesky" | custom-call | tf_op jit(solution)/shard_map/jit(cholesky)/cholesky | solution.py:39
  138.7 0.6 compare_reduce_fusion.3
  139.4 0.7 fusion.24
  140.1 4.9 %custom-call.21 = f32[1,64,64]{1,2,0:T(8,128)S(1)} custom-call(f32[1,64,64]{2,1,0:T(8,128)S(1)} %fusion.24), custom_call_target="InvertDiagBlocksLowerTriangular" | custom-call | tf_op jit(solution)/shard_map/triangular_solve/custom-call.4 | solution.py:42
  144.9 0.3 fusion.40
  145.2 0.2 convolution_bitcast_fusion.3
  145.4 0.7 gather_fusion.2
  146.1 0.7 multiply_reduce_fusion.2
  146.8 0.3 fusion.67
  147.0 1.5 collective-permute-start.2
  149.2 0.2 convolution_add_fusion.2
  149.5 5.8 %cholesky.111 = f32[64,64]{1,0:T(8,128)S(1)} custom-call(f32[64,64]{1,0:T(8,128)S(1)} %fusion.39), custom_call_target="Cholesky" | custom-call | tf_op jit(solution)/shard_map/jit(cholesky)/cholesky | solution.py:39
  155.4 0.6 compare_reduce_fusion.2
  156.1 0.7 fusion.25
  156.7 4.9 %custom-call.23 = f32[1,64,64]{1,2,0:T(8,128)S(1)} custom-call(f32[1,64,64]{2,1,0:T(8,128)S(1)} %fusion.25), custom_call_target="InvertDiagBlocksLowerTriangular" | custom-call | tf_op jit(solution)/shard_map/triangular_solve/custom-call.4 | solution.py:42
  161.6 0.3 fusion.36
  162.1 0.7 gather_fusion.3
  162.8 0.7 multiply_reduce_fusion.1
  163.5 0.3 fusion.66
  163.7 2.5 %collective-permute-start.3 = (f32[64,256]{1,0:T(8,128)S(1)}, f32[64,256]{1,0:T(8,128)S(1)}, u32[]{:S(2)}, u32[]{:S(2)}) collective-permute-start(f32[64,256]{1,0:T(8,128)S(1)} %get-tuple-element.27), channel_id=1, source_target_pairs={{0,16},{2,18},{4,20},{6,22},{8,24},{10,26},{12,28},{14,30},{16,0},... | collective-permute-start | bytes 196616 | tf_op jit(solution)/shard_map/ppermute | solution.py:14
  166.8 0.2 convolution_add_fusion.1
  167.1 5.8 %cholesky.122 = f32[64,64]{1,0:T(8,128)S(1)} custom-call(f32[64,64]{1,0:T(8,128)S(1)} %fusion.35), custom_call_target="Cholesky" | custom-call | tf_op jit(solution)/shard_map/jit(cholesky)/cholesky | solution.py:39
  173.0 0.6 compare_reduce_fusion.1
  173.7 0.7 fusion.26
  174.3 4.9 %custom-call.25 = f32[1,64,64]{1,2,0:T(8,128)S(1)} custom-call(f32[1,64,64]{2,1,0:T(8,128)S(1)} %fusion.26), custom_call_target="InvertDiagBlocksLowerTriangular" | custom-call | tf_op jit(solution)/shard_map/triangular_solve/custom-call.4 | solution.py:42
  179.2 0.3 fusion.32
  179.7 0.7 gather_fusion.4
  180.4 1.3 select_bitcast_fusion
  181.7 0.3 fusion.20
  182.6 0.3 convolution_add_fusion
  183.0 5.8 %cholesky.133 = f32[64,64]{1,0:T(8,128)S(1)} custom-call(f32[64,64]{1,0:T(8,128)S(1)} %fusion.31), custom_call_target="Cholesky" | custom-call | tf_op jit(solution)/shard_map/jit(cholesky)/cholesky | solution.py:39
  188.9 0.6 compare_reduce_fusion
  189.5 0.7 fusion.27
  190.2 4.9 %custom-call.27 = f32[1,64,64]{1,2,0:T(8,128)S(1)} custom-call(f32[1,64,64]{2,1,0:T(8,128)S(1)} %fusion.27), custom_call_target="InvertDiagBlocksLowerTriangular" | custom-call | tf_op jit(solution)/shard_map/triangular_solve/custom-call.4 | solution.py:42
  195.1 0.3 fusion.28
  195.5 0.7 maximum_bitcast_fusion
  (53 shorter events, 1.6 us)
Async XLA Ops:
  7.2 0.7 copy-start.4
  7.2 102.5 %all-reduce.2.cloned.1.call-start = ((), (), s32[]{:S(2)}) async-start(), calls=%async_computation | async-start | bytes 1048576 | tf_op jit(solution)/shard_map/psum | solution.py:66
  50.3 0.7 copy-start.1
  51.0 0.7 copy-start.2
  93.1 0.7 copy-start.5
  93.8 0.7 copy-start.3
  110.9 16.4 %copy-start = (f32[512,256]{0,1:T(8,128)S(1)}, f32[512,256]{0,1:T(8,128)}, u32[]{:S(2)}) copy-start(f32[512,256]{0,1:T(8,128)} %all-reduce.2.cloned.1.call-done) | copy-start | bytes 1572868
  112.3 16.5 %collective-permute-start = (f32[64,256]{1,0:T(8,128)S(1)}, f32[64,256]{1,0:T(8,128)S(1)}, u32[]{:S(2)}, u32[]{:S(2)}) collective-permute-start(f32[64,256]{1,0:T(8,128)S(1)} %get-tuple-element.37), channel_id=1, source_target_pairs={{0,2},{2,0},{4,6},{6,4},{8,10},{10,8},{12,14},{14,12},{16,18},{18,... | collective-permute-start | bytes 196616 | tf_op jit(solution)/shard_map/ppermute | solution.py:14
  130.4 15.0 %collective-permute-start.1 = (f32[64,256]{1,0:T(8,128)S(1)}, f32[64,256]{1,0:T(8,128)S(1)}, u32[]{:S(2)}, u32[]{:S(2)}) collective-permute-start(f32[64,256]{1,0:T(8,128)S(1)} %get-tuple-element.23), channel_id=1, source_target_pairs={{0,4},{2,6},{4,0},{6,2},{8,12},{10,14},{12,8},{14,10},{16,20},{18,... | collective-permute-start | bytes 196616 | tf_op jit(solution)/shard_map/ppermute | solution.py:14
  147.0 15.0 %collective-permute-start.2 = (f32[64,256]{1,0:T(8,128)S(1)}, f32[64,256]{1,0:T(8,128)S(1)}, u32[]{:S(2)}, u32[]{:S(2)}) collective-permute-start(f32[64,256]{1,0:T(8,128)S(1)} %get-tuple-element.25), channel_id=1, source_target_pairs={{0,8},{2,10},{4,12},{6,14},{8,0},{10,2},{12,4},{14,6},{16,24},{18,... | collective-permute-start | bytes 196616 | tf_op jit(solution)/shard_map/ppermute | solution.py:14
  163.7 15.9 %collective-permute-start.3 = (f32[64,256]{1,0:T(8,128)S(1)}, f32[64,256]{1,0:T(8,128)S(1)}, u32[]{:S(2)}, u32[]{:S(2)}) collective-permute-start(f32[64,256]{1,0:T(8,128)S(1)} %get-tuple-element.27), channel_id=1, source_target_pairs={{0,16},{2,18},{4,20},{6,22},{8,24},{10,26},{12,28},{14,30},{16,0},... | collective-permute-start | bytes 196616 | tf_op jit(solution)/shard_map/ppermute | solution.py:14
Sparse Core Ops, SparseCore 0:
  93.3 16.3 all-reduce.1
where the time goes:
time: 203 us
  blocking collectives  78.3 us (39%)
  other arithmetic  66.2 us (33%)
  between operations  17.8 us (9%)
  waiting for transfers between devices  15.1 us (7%)
  matrix products  9.95 us (5%)
  local copies, waits for them, and re-layouts  8.37 us (4%)
  starting transfers between devices  7.37 us (4%)
    all_gather x1, blocking collectives, body(): sources = lax.all_gather(panel_points, 'rows', axis=1, tiled=True)  42.5 us
    all_gather x1, blocking collectives, body(): vectors = lax.all_gather(test_vectors, 'rows', axis=1, tiled=True)  35.8 us
    another operation x15, other arithmetic, interpolate(): factor = jnp.linalg.cholesky(gram_matrix)  32.7 us
    another operation x10, other arithmetic, interpolate(): lax.linalg.triangular_solve(factor, middle, left_side=True, lower=True, t...  27.8 us
    psum x1, waiting for transfers between devices, body(): samples = lax.psum(running, 'cols')  15.1 us
    ppermute x4, starting transfers between devices, from_partner(): lax.ppermute(shard, axis, [(i, i ^ 1 << bit) for i in range(lax.axis_size...  7.33 us
  transfers between devices with their start and end apart: 5, of which 1 were waited for; matrix products, arithmetic and copies ran while one was open for 26% of the time, Pallas kernels for 0%

commit v1 on v0

--- a/solution.py
+++ b/solution.py
@@ -8,6 +8,32 @@
 SMOOTH = 0.05
 RIDGE = 0.1
 EPSILON = 1e-05
+
+
+def _supply_things(incoming_x, row_dim):
+    incoming_x = jnp.moveaxis(incoming_x, 0, row_dim)
+    big = incoming_x.shape
+    return incoming_x.reshape(*big[:row_dim], big[row_dim] * big[row_dim + 1], *big[row_dim + 2 :])
+
+
+def carry_strips_all(inp, group_axis):
+    v_next = lax.axis_size(group_axis)
+    moved, piece_next = (v_next, lax.axis_index(group_axis))
+    r_now, p_next = (inp[None], 1)
+    while p_next < moved:
+        series = []
+        for u in range(moved):
+            series.append((u, u ^ p_next))
+        odd = lax.ppermute(r_now, group_axis, series)
+        v_now = piece_next & p_next == 0
+        r_now = jnp.concatenate([jnp.where(v_now, r_now, odd), jnp.where(v_now, odd, r_now)])
+        p_next *= 2
+    return r_now
+
+
+def work_sectors(m, x_local, pos_dim):
+    b_now = carry_strips_all(m, x_local)
+    return _supply_things(b_now, pos_dim)
 
 
 def from_partner(shard, axis, bit):
@@ -48,7 +74,7 @@
     level_count = node_skeleton.shape[1]
     zero_sum = jnp.zeros((rows_here, 2 * vec_count), jnp.float32)
     running = zero_sum
-    vectors = lax.all_gather(test_vectors, "rows", axis=1, tiled=True)
+    vectors = work_sectors(test_vectors, "rows", 1)
     sources = lax.all_gather(panel_points, "rows", axis=1, tiled=True)
     piece_width = vectors.shape[1]
     block_width = math.gcd(piece_width, 512)

time: 203 us -> 179 us (0.88)
  blocking collectives: 78.3 us -> 40.1 us
  waiting for transfers between devices: 15.1 us -> 26.1 us
  starting transfers between devices: 7.37 us -> 10.6 us
    all_gather x1 -> x0, blocking collectives: 35.8 us -> none  [body(): vectors = lax.all_gather(test_vectors, 'rows', axis=1, tiled=True)]
    ppermute x0 -> x4, waiting for transfers between devices: none -> 11.5 us  [carry_strips_all(): odd = lax.ppermute(r_now, group_axis, series)]
    ppermute x0 -> x4, starting transfers between devices: none -> 3.24 us  [carry_strips_all(): odd = lax.ppermute(r_now, group_axis, series)]
    all_gather x1, blocking collectives: 42.5 us -> 40.1 us  [body(): sources = lax.all_gather(panel_points, 'rows', axis=1, tiled=True)]
  transfers between devices with their start and end apart: 5 -> 9, of which waited for: 1 -> 4; matrix products, arithmetic and copies ran while one was open for 26% -> 29% of each run, Pallas kernels for 0% -> 0%
where the time goes in v1:
time: 179 us
  other arithmetic  66.4 us (37%)
  blocking collectives  40.1 us (22%)
  waiting for transfers between devices  26.1 us (15%)
  between operations  17.8 us (10%)
  starting transfers between devices  10.6 us (6%)
  matrix products  9.95 us (6%)
  local copies, waits for them, and re-layouts  7.66 us (4%)
    all_gather x1, blocking collectives, body(): sources = lax.all_gather(panel_points, 'rows', axis=1, tiled=True)  40.1 us
    another operation x15, other arithmetic, interpolate(): factor = jnp.linalg.cholesky(gram_matrix)  32.8 us
    another operation x10, other arithmetic, interpolate(): lax.linalg.triangular_solve(factor, middle, left_side=True, lower=True, t...  27.8 us
    psum x1, waiting for transfers between devices, body(): samples = lax.psum(running, 'cols')  14.6 us
    ppermute x4, waiting for transfers between devices, carry_strips_all(): odd = lax.ppermute(r_now, group_axis, series)  11.5 us
    ppermute x4, starting transfers between devices, from_partner(): lax.ppermute(shard, axis, [(i, i ^ 1 << bit) for i in range(lax.axis_size...  7.32 us
  transfers between devices with their start and end apart: 9, of which 4 were waited for; matrix products, arithmetic and copies ran while one was open for 29% of the time, Pallas kernels for 0%

profile of v1, /device:TPU:0, one launch (start us, length us, event | category | flops | bytes accessed | tf_op | source)
XLA Modules:
  0.0 178.7 jit_solution(288993253536378134)
XLA Ops:
  7.2 3.0 %collective-permute-start = (bf16[1,128,16]{1,2,0:T(8,128)(2,1)}, bf16[1,128,16]{1,2,0:T(8,128)(2,1)S(1)}, u32[]{:S(2)}, u32[]{:S(2)}) collective-permute-start(bf16[1,128,16]{1,2,0:T(8,128)(2,1)} %bitcast.138), channel_id=1, source_target_pairs={{0,2},{2,0},{4,6},{6,4},{8,10},{10,8},{12,14},{14,12},{16,18},{18,... | collective-permute-start | bytes 12296 | tf_op jit(solution)/shard_map/ppermute | solution.py:27
  10.3 40.1 %all-gather = bf16[16,16,3]{1,2,0:T(4,128)(2,1)S(1)} all-gather(bf16[1,16,3]{1,2,0:T(4,128)(2,1)S(1)} %bitcast.145), channel_id=1, replica_groups=mesh['rows'=16,'cols'=2] {'rows'}, dimensions={0}, use_global_device_ids=true | all-gather | bytes 1632 | tf_op jit(solution)/shard_map/all_gather | solution.py:78
  50.5 0.6 copy-done.1
  51.1 0.7 copy-done.3
  51.8 0.7 copy-done.2
  52.5 0.6 copy-done.5
  53.1 3.1 %collective-permute-done.1 = bf16[2,128,16]{1,2,0:T(8,128)(2,1)S(1)} collective-permute-done((bf16[2,128,16]{1,2,0:T(8,128)(2,1)S(1)}, bf16[2,128,16]{1,2,0:T(8,128)(2,1)S(1)}, u32[]{:S(2)}, u32[]{:S(2)}) %collective-permute-start.1) | collective-permute-done | bytes 8224 | tf_op jit(solution)/shard_map/ppermute | solution.py:27
  56.3 3.7 %collective-permute-done.2 = bf16[4,128,16]{1,2,0:T(8,128)(2,1)S(1)} collective-permute-done((bf16[4,128,16]{1,2,0:T(8,128)(2,1)S(1)}, bf16[4,128,16]{1,2,0:T(8,128)(2,1)S(1)}, u32[]{:S(2)}, u32[]{:S(2)}) %collective-permute-start.2) | collective-permute-done | bytes 16416 | tf_op jit(solution)/shard_map/ppermute | solution.py:27
  60.1 4.8 %collective-permute-done.3 = bf16[8,128,16]{1,2,0:T(8,128)(2,1)S(1)} collective-permute-done((bf16[8,128,16]{1,2,0:T(8,128)(2,1)S(1)}, bf16[8,128,16]{1,2,0:T(8,128)(2,1)S(1)}, u32[]{:S(2)}, u32[]{:S(2)}) %collective-permute-start.3) | collective-permute-done | bytes 32800 | tf_op jit(solution)/shard_map/ppermute | solution.py:27
  64.9 2.4 %fusion = f32[512,128]{0,1:T(8,128)S(1)} fusion(bf16[128,256]{0,1:T(8,128)(2,1)S(1)} %bitcast.135, f32[256]{0:T(256)S(1)} %bitcast.148, f32[512]{0:T(512)S(1)} %bitcast.141, f32[256]{0:T(256)S(1)} %bitcast.150, f32[512]{0:T(512)S(1)} %bitcast.143, f32[256]{0:T(256)S(1)} %bitcast.146, f32[512]{0:T(512)S(1)} %bitcast.139), kind=kOutput, calls=%fused_computation.18 | convolution fusion | flops 35127296 | bytes 336896 | tf_op jit(solution)/shard_map/while/body/eval_jaxpr/dot_general | solution.py:56
  67.3 2.4 %fusion.1 = f32[512,128]{0,1:T(8,128)S(1)} fusion(bf16[128,256]{0,1:T(8,128)(2,1)S(1)} %bitcast.136, f32[256]{0:T(256)S(1)} %bitcast.149, f32[512]{0:T(512)S(1)} %bitcast.142, f32[256]{0:T(256)S(1)} %bitcast.151, f32[512]{0:T(512)S(1)} %bitcast.144, f32[256]{0:T(256)S(1)} %bitcast.147, f32[512]{0:T(512)S(1)} %bitcast.140), kind=kOutput, calls=%fused_computation.19 | convolution fusion | flops 35127296 | bytes 336896 | tf_op jit(solution)/shard_map/while/body/eval_jaxpr/dot_general | solution.py:57
  69.7 0.8 pad_maximum_fusion
  70.6 14.6 %all-reduce.2.cloned.1.call-done = f32[512,256]{0,1:T(8,128)} async-done(((f32[512,256]{0,1:T(8,128)}), f32[512,256]{0,1:T(8,128)}) %all-reduce.2.cloned.1.call-update) | async-done | bytes 524304 | tf_op jit(solution)/shard_map/psum | solution.py:92
  85.2 1.2 copy.53
  86.5 0.7 gather_fusion
  87.1 0.7 multiply_reduce_fusion.4
  87.8 1.8 collective-permute-start.4
  90.2 0.2 convolution_add_fusion.4
  90.5 5.8 %cholesky.89 = f32[64,64]{1,0:T(8,128)S(1)} custom-call(f32[64,64]{1,0:T(8,128)S(1)} %fusion.48), custom_call_target="Cholesky" | custom-call | tf_op jit(solution)/shard_map/jit(cholesky)/cholesky | solution.py:65
  96.6 0.6 compare_reduce_fusion.4
  97.2 0.7 fusion.23
  98.0 4.9 %custom-call.13 = f32[1,64,64]{1,2,0:T(8,128)S(1)} custom-call(f32[1,64,64]{2,1,0:T(8,128)S(1)} %copy.58), custom_call_target="InvertDiagBlocksLowerTriangular" | custom-call | tf_op jit(solution)/shard_map/triangular_solve | solution.py:68
  102.9 0.3 fusion.2
  103.2 0.3 fusion.46
  103.4 0.8 fusion.44
  104.3 0.7 gather_fusion.1
  105.0 0.7 multiply_reduce_fusion.3
  105.6 0.3 fusion.68
  105.9 1.5 collective-permute-start.5
  108.4 5.8 %cholesky.100 = f32[64,64]{1,0:T(8,128)S(1)} custom-call(f32[64,64]{1,0:T(8,128)S(1)} %fusion.43), custom_call_target="Cholesky" | custom-call | tf_op jit(solution)/shard_map/jit(cholesky)/cholesky | solution.py:65
  114.3 0.6 compare_reduce_fusion.3
  114.9 0.7 fusion.24
  115.6 4.9 %custom-call.21 = f32[1,64,64]{1,2,0:T(8,128)S(1)} custom-call(f32[1,64,64]{2,1,0:T(8,128)S(1)} %fusion.24), custom_call_target="InvertDiagBlocksLowerTriangular" | custom-call | tf_op jit(solution)/shard_map/triangular_solve/custom-call.4 | solution.py:68
  120.5 0.3 fusion.40
  121.0 0.7 gather_fusion.2
  121.6 0.7 multiply_reduce_fusion.2
  122.3 0.3 fusion.67
  122.6 1.5 collective-permute-start.6
  124.8 0.2 convolution_add_fusion.2
  125.1 6.0 %cholesky.111 = f32[64,64]{1,0:T(8,128)S(1)} custom-call(f32[64,64]{1,0:T(8,128)S(1)} %fusion.39), custom_call_target="Cholesky" | custom-call | tf_op jit(solution)/shard_map/jit(cholesky)/cholesky | solution.py:65
  131.1 0.6 compare_reduce_fusion.2
  131.7 0.7 fusion.25
  132.4 4.9 %custom-call.23 = f32[1,64,64]{1,2,0:T(8,128)S(1)} custom-call(f32[1,64,64]{2,1,0:T(8,128)S(1)} %fusion.25), custom_call_target="InvertDiagBlocksLowerTriangular" | custom-call | tf_op jit(solution)/shard_map/triangular_solve/custom-call.4 | solution.py:68
  137.3 0.3 fusion.36
  137.8 0.7 gather_fusion.3
  138.4 0.7 multiply_reduce_fusion.1
  139.1 0.3 fusion.66
  139.4 2.5 %collective-permute-start.7 = (f32[64,256]{1,0:T(8,128)S(1)}, f32[64,256]{1,0:T(8,128)S(1)}, u32[]{:S(2)}, u32[]{:S(2)}) collective-permute-start(f32[64,256]{1,0:T(8,128)S(1)} %get-tuple-element.27), channel_id=1, source_target_pairs={{0,16},{2,18},{4,20},{6,22},{8,24},{10,26},{12,28},{14,30},{16,0},... | collective-permute-start | bytes 196616 | tf_op jit(solution)/shard_map/ppermute | solution.py:40
  142.5 0.2 convolution_add_fusion.1
  142.8 5.8 %cholesky.122 = f32[64,64]{1,0:T(8,128)S(1)} custom-call(f32[64,64]{1,0:T(8,128)S(1)} %fusion.35), custom_call_target="Cholesky" | custom-call | tf_op jit(solution)/shard_map/jit(cholesky)/cholesky | solution.py:65
  148.7 0.6 compare_reduce_fusion.1
  149.3 0.7 fusion.26
  150.0 4.9 %custom-call.25 = f32[1,64,64]{1,2,0:T(8,128)S(1)} custom-call(f32[1,64,64]{2,1,0:T(8,128)S(1)} %fusion.26), custom_call_target="InvertDiagBlocksLowerTriangular" | custom-call | tf_op jit(solution)/shard_map/triangular_solve/custom-call.4 | solution.py:68
  154.9 0.3 fusion.32
  155.4 0.7 gather_fusion.4
  156.0 1.3 select_bitcast_fusion
  157.3 0.3 fusion.20
  158.3 0.3 convolution_add_fusion
  158.7 5.8 %cholesky.133 = f32[64,64]{1,0:T(8,128)S(1)} custom-call(f32[64,64]{1,0:T(8,128)S(1)} %fusion.31), custom_call_target="Cholesky" | custom-call | tf_op jit(solution)/shard_map/jit(cholesky)/cholesky | solution.py:65
  164.5 0.6 compare_reduce_fusion
  165.2 0.7 fusion.27
  165.8 4.9 %custom-call.27 = f32[1,64,64]{1,2,0:T(8,128)S(1)} custom-call(f32[1,64,64]{2,1,0:T(8,128)S(1)} %fusion.27), custom_call_target="InvertDiagBlocksLowerTriangular" | custom-call | tf_op jit(solution)/shard_map/triangular_solve/custom-call.4 | solution.py:68
  170.7 0.3 fusion.28
  171.2 0.7 maximum_bitcast_fusion
  (68 shorter events, 2.3 us)
Async XLA Ops:
  7.2 78.0 %all-reduce.2.cloned.1.call-start = ((), (), s32[]{:S(2)}) async-start(), calls=%async_computation | async-start | bytes 1048576 | tf_op jit(solution)/shard_map/psum | solution.py:92
  7.2 3.0 %copy-start.4 = (bf16[3,16]{1,0:T(4,128)(2,1)S(1)}, bf16[3,16]{1,0:T(4,128)(2,1)}, u32[]{:S(2)}) copy-start(bf16[3,16]{1,0:T(4,128)(2,1)} %param.13) | copy-start | bytes 292
  7.2 44.6 %collective-permute-start = (bf16[1,128,16]{1,2,0:T(8,128)(2,1)}, bf16[1,128,16]{1,2,0:T(8,128)(2,1)S(1)}, u32[]{:S(2)}, u32[]{:S(2)}) collective-permute-start(bf16[1,128,16]{1,2,0:T(8,128)(2,1)} %bitcast.138), channel_id=1, source_target_pairs={{0,2},{2,0},{4,6},{6,4},{8,10},{10,8},{12,14},{14,12},{16,18},{18,... | collective-permute-start | bytes 12296 | tf_op jit(solution)/shard_map/ppermute | solution.py:27
  50.4 0.7 copy-start.1
  51.1 0.7 copy-start.3
  51.8 0.7 copy-start.2
  52.5 0.7 copy-start.5
  52.5 3.7 %collective-permute-start.1 = (bf16[2,128,16]{1,2,0:T(8,128)(2,1)S(1)}, bf16[2,128,16]{1,2,0:T(8,128)(2,1)S(1)}, u32[]{:S(2)}, u32[]{:S(2)}) collective-permute-start(bf16[2,128,16]{1,2,0:T(8,128)(2,1)S(1)} %pad_maximum_fusion.8), channel_id=1, source_target_pairs={{0,4},{2,6},{4,0},{6,2},{8,12},{10,14},{12,8},{14,10},{16,20},{18,... | collective-permute-start | bytes 24584 | tf_op jit(solution)/shard_map/ppermute | solution.py:27
  56.2 3.8 %collective-permute-start.2 = (bf16[4,128,16]{1,2,0:T(8,128)(2,1)S(1)}, bf16[4,128,16]{1,2,0:T(8,128)(2,1)S(1)}, u32[]{:S(2)}, u32[]{:S(2)}) collective-permute-start(bf16[4,128,16]{1,2,0:T(8,128)(2,1)S(1)} %pad_maximum_fusion.7), channel_id=1, source_target_pairs={{0,8},{2,10},{4,12},{6,14},{8,0},{10,2},{12,4},{14,6},{16,24},{18,... | collective-permute-start | bytes 49160 | tf_op jit(solution)/shard_map/ppermute | solution.py:27
  60.0 4.9 %collective-permute-start.3 = (bf16[8,128,16]{1,2,0:T(8,128)(2,1)S(1)}, bf16[8,128,16]{1,2,0:T(8,128)(2,1)S(1)}, u32[]{:S(2)}, u32[]{:S(2)}) collective-permute-start(bf16[8,128,16]{1,2,0:T(8,128)(2,1)S(1)} %pad_maximum_fusion.6), channel_id=1, source_target_pairs={{0,16},{2,18},{4,20},{6,22},{8,24},{10,26},{12,28},{14,30},{16,0},... | collective-permute-start | bytes 98312 | tf_op jit(solution)/shard_map/ppermute | solution.py:27
  86.4 16.4 %copy-start = (f32[512,256]{0,1:T(8,128)S(1)}, f32[512,256]{0,1:T(8,128)}, u32[]{:S(2)}) copy-start(f32[512,256]{0,1:T(8,128)} %all-reduce.2.cloned.1.call-done) | copy-start | bytes 1572868
  87.8 16.5 %collective-permute-start.4 = (f32[64,256]{1,0:T(8,128)S(1)}, f32[64,256]{1,0:T(8,128)S(1)}, u32[]{:S(2)}, u32[]{:S(2)}) collective-permute-start(f32[64,256]{1,0:T(8,128)S(1)} %get-tuple-element.37), channel_id=1, source_target_pairs={{0,2},{2,0},{4,6},{6,4},{8,10},{10,8},{12,14},{14,12},{16,18},{18,... | collective-permute-start | bytes 196616 | tf_op jit(solution)/shard_map/ppermute | solution.py:40
  105.9 15.0 %collective-permute-start.5 = (f32[64,256]{1,0:T(8,128)S(1)}, f32[64,256]{1,0:T(8,128)S(1)}, u32[]{:S(2)}, u32[]{:S(2)}) collective-permute-start(f32[64,256]{1,0:T(8,128)S(1)} %get-tuple-element.23), channel_id=1, source_target_pairs={{0,4},{2,6},{4,0},{6,2},{8,12},{10,14},{12,8},{14,10},{16,20},{18,... | collective-permute-start | bytes 196616 | tf_op jit(solution)/shard_map/ppermute | solution.py:40
  122.6 15.1 %collective-permute-start.6 = (f32[64,256]{1,0:T(8,128)S(1)}, f32[64,256]{1,0:T(8,128)S(1)}, u32[]{:S(2)}, u32[]{:S(2)}) collective-permute-start(f32[64,256]{1,0:T(8,128)S(1)} %get-tuple-element.25), channel_id=1, source_target_pairs={{0,8},{2,10},{4,12},{6,14},{8,0},{10,2},{12,4},{14,6},{16,24},{18,... | collective-permute-start | bytes 196616 | tf_op jit(solution)/shard_map/ppermute | solution.py:40
  139.4 15.9 %collective-permute-start.7 = (f32[64,256]{1,0:T(8,128)S(1)}, f32[64,256]{1,0:T(8,128)S(1)}, u32[]{:S(2)}, u32[]{:S(2)}) collective-permute-start(f32[64,256]{1,0:T(8,128)S(1)} %get-tuple-element.27), channel_id=1, source_target_pairs={{0,16},{2,18},{4,20},{6,22},{8,24},{10,26},{12,28},{14,30},{16,0},... | collective-permute-start | bytes 196616 | tf_op jit(solution)/shard_map/ppermute | solution.py:40
Sparse Core Ops, SparseCore 0:
  70.7 14.4 all-reduce.1
